TPU v7x, 32 devices: a whole 2x2x4 slice. The times are simulated.
32 devices in a mesh: groups: 2 (over x), tm: 16 (over z, y, core).
Axes of the slice: x: 2, y: 2, z: 4, core: 2. Of those that a mesh axis runs over, the one named last changes fastest.
Arguments:
- queries: bfloat16 [6144, 2560], P(('groups', 'tm')), parts along dimension 0, may hold values from -6 to 6
- keys: bfloat16 [6144, 2560], P(('groups', 'tm')), parts along dimension 0, may hold values from -6 to 6
- values: bfloat16 [6144, 2560], P(('groups', 'tm')), parts along dimension 0, may hold values from -6 to 6
- q_gain: float32 [2560], replicated, may hold values from 0.5 to 1.5
- k_gain: float32 [2560], replicated, may hold values from 0.5 to 1.5
- out_weight: bfloat16 [2560, 5120], P('tm'), may hold values from -0.125 to 0.125
- out_gate: float32 [5120], replicated, may hold values from 0.5 to 2
- reach: int32 [32, 2], P(('groups', 'tm')), parts along dimension 0, may hold values from 0 to 1
Outputs:
- mixed: bfloat16 [6144, 5120], P(('groups', 'tm')), parts along dimension 0
There are 2 independent parts, one for each index of `groups`. A program takes and returns all parts, laid end to end along the dimension named above; an argument that names none is the same for every part. Nothing has to cross between parts.
Inputs may be any that keep to these rules, and one draw needn't show every extreme that they name: `reach`: requests past the first or last tile are ignored.
All inputs are finite; a program needn't handle non-finite values.
Results may differ from a plain program's by a relative error of at most 0.0076.
Values may be sent and summed in bfloat16 or wider, within the bound.
A program may use at most 128 MiB of HBM per device.

v0:
```python
import jax
import jax.numpy as jnp
from jax import lax
from jax.sharding import PartitionSpec as P

HD = 128
TT = 4
TH = 6
TW = 8


def shifted(shard, axis, by):
    peers = lax.axis_size(axis)
    pairs = [(i, i + by) for i in range(peers) if 0 <= i + by < peers]
    return lax.ppermute(shard, axis, pairs)


def rms_scaled(block, gain):
    values32 = block.astype(jnp.float32)
    inverse = lax.rsqrt(jnp.mean(values32 * values32, axis=-1, keepdims=True) + 1e-06)
    return (values32 * inverse * gain).astype(jnp.bfloat16)


def local(queries, keys, values, q_gain, k_gain, out_weight, out_gate, reach):
    tile = TT * TH * TW
    rows = queries.shape[0]
    chans = queries.shape[1]
    heads = chans // HD
    count = rows // tile
    scale = HD ** (-0.5)
    q_norm = rms_scaled(queries, q_gain)
    k_norm = rms_scaled(keys, k_gain)
    before_k, before_v = shifted((k_norm, values), "tm", 1)
    after_k, after_v = shifted((k_norm, values), "tm", -1)
    key_buffer = jnp.concatenate([before_k, k_norm, after_k], axis=0).reshape(
        count + 2, tile, heads, HD
    )
    val_buffer = jnp.concatenate([before_v, values, after_v], axis=0).reshape(
        count + 2, tile, heads, HD
    )
    position = lax.axis_index("tm")
    first_tile = position * count
    total_tiles = lax.axis_size("tm") * count
    global_tile = first_tile + jnp.arange(count, dtype=jnp.int32)
    valid = jnp.stack(
        [
            (reach[:, 0] == 1) & (global_tile > 0),
            global_tile >= 0,
            (reach[:, 1] == 1) & (global_tile < total_tiles - 1),
        ],
        axis=1,
    )
    query_tiles = q_norm.reshape(count, tile, heads, HD)
    seen_k = jnp.stack([key_buffer[offset : offset + count] for offset in range(3)], axis=1)
    seen_v = jnp.stack([val_buffer[offset : offset + count] for offset in range(3)], axis=1)
    logits = (
        jnp.einsum("nqhd,nokhd->nhqok", query_tiles, seen_k, preferred_element_type=jnp.float32)
        * scale
    )
    logits = jnp.where(valid[:, None, None, :, None], logits, -1e30)
    logits = logits.reshape(count, heads, tile, 3 * tile)
    top = jnp.max(logits, axis=-1, keepdims=True)
    expo = jnp.exp(logits - top)
    weights = (expo / jnp.sum(expo, axis=-1, keepdims=True)).astype(jnp.bfloat16)
    attended = jnp.einsum(
        "nhqk,nkhd->nqhd",
        weights,
        seen_v.reshape(count, 3 * tile, heads, HD),
        preferred_element_type=jnp.float32,
    ).astype(jnp.bfloat16)
    attended = attended.reshape(rows, chans)
    full_weight = lax.all_gather(out_weight, "tm", axis=0, tiled=True)
    projected = jnp.dot(attended, full_weight, preferred_element_type=jnp.float32)
    return (out_gate * projected).astype(jnp.bfloat16)


def solution(mesh):
    return jax.shard_map(
        local,
        mesh=mesh,
        in_specs=(
            P(("groups", "tm"), None),
            P(("groups", "tm"), None),
            P(("groups", "tm"), None),
            P(),
            P(),
            P("tm", None),
            P(),
            P(("groups", "tm"), None),
        ),
        out_specs=P(("groups", "tm"), None),
        check_vma=False,
    )
```

profile of v0, /device:TPU:27, one launch (start us, length us, event | category | flops | bytes accessed | tf_op | source)
XLA Modules:
  0.0 202.7 jit_solution(11805782908131688679)
XLA Ops:
  6.5 0.0 all-gather.2.cloned.1.call-start
  6.5 0.7 all-gather.2.cloned.1.call-update
  7.3 1.5 fusion.5
  8.7 0.0 copy-done.1
  8.8 0.0 copy-start.6
  8.8 1.0 fusion.7
  9.8 3.7 %collective-permute-start.2 = (bf16[192,2560]{1,0:T(8,128)(2,1)S(1)}, bf16[192,2560]{1,0:T(8,128)(2,1)}, u32[]{:S(2)}, u32[]{:S(2)}) collective-permute-start(bf16[192,2560]{1,0:T(8,128)(2,1)S(1)} %fusion.7), channel_id=1, source_target_pairs={{0,1},{1,2},{2,3},{3,4},{4,5},{5,6},{6,7},{7,8},{8,9},{9,10},{10,1... | collective-permute-start | bytes 2949128 | tf_op jit(solution)/shard_map/ppermute | solution.py:15
  13.5 1.9 collective-permute-start.3
  15.4 3.6 %collective-permute-start = (bf16[192,2560]{1,0:T(8,128)(2,1)}, bf16[192,2560]{1,0:T(8,128)(2,1)}, u32[]{:S(2)}, u32[]{:S(2)}) collective-permute-start(bf16[192,2560]{1,0:T(8,128)(2,1)} %param.10), channel_id=1, source_target_pairs={{0,1},{1,2},{2,3},{3,4},{4,5},{5,6},{6,7},{7,8},{8,9},{9,10},{10,1... | collective-permute-start | bytes 2949128 | tf_op jit(solution)/shard_map/ppermute | solution.py:15
  19.1 1.9 collective-permute-start.1
  21.0 0.7 stack.45
  21.7 1.7 stack.37
  23.3 0.0 copy-done.6
  23.4 0.6 fusion.17
  25.3 1.2 copy.16
  26.5 0.1 add_bitcast_fusion
  26.5 1.5 fusion.2
  28.0 11.8 %collective-permute-done.2 = bf16[192,2560]{1,0:T(8,128)(2,1)} collective-permute-done((bf16[192,2560]{1,0:T(8,128)(2,1)S(1)}, bf16[192,2560]{1,0:T(8,128)(2,1)}, u32[]{:S(2)}, u32[]{:S(2)}) %collective-permute-start.2) | collective-permute-done | bytes 983072 | tf_op jit(solution)/shard_map/ppermute | solution.py:15
  39.9 1.7 stack.44
  41.5 1.2 copy.15
  42.7 23.5 %collective-permute-done.3 = bf16[192,2560]{1,0:T(8,128)(2,1)} collective-permute-done((bf16[192,2560]{1,0:T(8,128)(2,1)S(1)}, bf16[192,2560]{1,0:T(8,128)(2,1)}, u32[]{:S(2)}, u32[]{:S(2)}) %collective-permute-start.3) | collective-permute-done | bytes 983072 | tf_op jit(solution)/shard_map/ppermute | solution.py:15
  66.2 1.7 stack.46
  67.8 0.2 copy.17
  68.0 0.0 copy-done.3
  68.0 0.0 copy-start.2
  68.1 0.0 copy-start.5
  68.1 1.6 pad_maximum_fusion.1
  69.7 0.0 copy-done.2
  69.7 0.0 copy-done.5
  69.7 6.1 %fusion.13 = f32[20,192,576]{1,2,0} fusion(bf16[20,128,576]{1,2,0:T(8,128)(2,1)S(1)} %bitcast.38, bf16[192,2560]{1,0:T(8,128)(2,1)S(1)} %copy-done.2, f32[2560]{0:T(1024)S(1)} %copy-done.5, f32[192]{0:T(256)S(1)} %add_rsqrt_fusion.1), kind=kOutput, calls=%fused_computation.23 | convolution fusion | flops 568197120 | bytes 12790528
  75.8 12.3 %fusion.16 = (f32[20,192]{1,0:T(8,128)}, f32[20,192,3,192]{1,3,2,0:T(8,128)}) fusion(f32[20,192,3,192]{1,3,2,0:T(8,128)} %bitcast.37, pred[3]{0:T(512)(128)(4,1)S(1)} %add_bitcast_fusion), kind=kLoop, calls=%fused_computation.29 | loop fusion | flops 6631680 | bytes 17710084 | tf_op jit(solution)/shard_map/reduce_max | solution.py:62
  88.1 11.7 %copy.19 = f32[20,192,576]{2,1,0:T(8,128)} copy(f32[20,192,576]{1,2,0:T(8,128)} %bitcast.36) | data formatting | bytes 17694720 | tf_op jit(solution)/shard_map/reshape | solution.py:61
  99.8 0.0 collective-permute-done
  99.8 1.7 stack.36
  101.5 0.0 collective-permute-done.1
  101.5 1.7 stack.38
  103.2 0.0 copy-start
  103.2 0.6 pad_maximum_fusion
  103.9 0.0 copy-start.4
  103.9 0.7 copy.14
  104.6 3.1 %copy-done = f32[20,192,3,192]{1,3,2,0:T(8,128)S(1)} copy-done((f32[20,192,3,192]{1,3,2,0:T(8,128)S(1)}, f32[20,192,3,192]{1,3,2,0:T(8,128)}, u32[]{:S(2)}) %copy-start) | copy-done | bytes 8847384
  107.7 0.0 copy-done.4
  107.7 1.8 exponential_reduce_fusion
  109.5 0.0 copy-start.7
  109.5 5.4 %fusion.9 = bf16[1,192,20,128]{3,1,2,0:T(8,128)(2,1)S(1)} fusion(bf16[576,20,128]{2,0,1:T(8,128)(2,1)S(1)} %bitcast.39, f32[20,192,576]{2,1,0:T(8,128)} %copy.19, f32[20,192]{1,0:T(8,128)S(1)} %exponential_reduce_fusion, f32[20,192]{1,0:T(8,128)S(1)} %copy-done.4), kind=kOutput, calls=%fused_computation.19 | convolution fusion | flops 573358080 | bytes 12810240 | tf_op jit(solution)/shard_map/nhqk,nkhd->nqhd/dot_general | solution.py:65
  114.9 0.7 copy.20
  115.6 67.5 %all-gather.2.cloned.1.call-done = bf16[2560,5120]{1,0:T(8,128)(2,1)} async-done(((bf16[160,5120]{1,0:T(8,128)(2,1)}), bf16[2560,5120]{1,0:T(8,128)(2,1)}) %all-gather.2.cloned.1.call-update) | async-done | bytes 26214416 | tf_op jit(solution)/shard_map/all_gather | solution.py:72
  183.1 12.7 %fusion = bf16[192,5120]{1,0:T(8,128)(2,1)} fusion(bf16[2560,5120]{1,0:T(8,128)(2,1)} %all-gather.2.cloned.1.call-done, f32[5120]{0:T(1024)S(1)} %copy-done.7, bf16[24,8,20,128]{3,2,1,0:T(8,128)(2,1)S(1)} %bitcast.40), kind=kOutput, calls=%fused_computation.4 | convolution fusion | flops 5035130880 | bytes 29184000 | tf_op jit(solution)/shard_map/dot_general | solution.py:73
  (5 shorter events, 0.0 us)
Async XLA Ops:
  6.5 2.2 %copy-start.1 = (bf16[192,2560]{1,0:T(8,128)(2,1)S(1)}, bf16[192,2560]{1,0:T(8,128)(2,1)}, u32[]{:S(2)}) copy-start(bf16[192,2560]{1,0:T(8,128)(2,1)} %param.9) | copy-start | bytes 2949124
  6.5 176.5 %all-gather.2.cloned.1.call-start = ((), (), s32[]{:S(2)}) async-start(), calls=%async_computation | async-start | bytes 27852800 | tf_op jit(solution)/shard_map/all_gather | solution.py:72
  8.8 14.6 %copy-start.6 = (s32[1,2]{1,0:T(1,128)S(1)}, s32[1,2]{1,0:T(1,128)}, u32[]{:S(2)}) copy-start(s32[1,2]{1,0:T(1,128)} %param.15) | copy-start | bytes 28
  9.8 30.1 %collective-permute-start.2 = (bf16[192,2560]{1,0:T(8,128)(2,1)S(1)}, bf16[192,2560]{1,0:T(8,128)(2,1)}, u32[]{:S(2)}, u32[]{:S(2)}) collective-permute-start(bf16[192,2560]{1,0:T(8,128)(2,1)S(1)} %fusion.7), channel_id=1, source_target_pairs={{0,1},{1,2},{2,3},{3,4},{4,5},{5,6},{6,7},{7,8},{8,9},{9,10},{10,1... | collective-permute-start | bytes 2949128 | tf_op jit(solution)/shard_map/ppermute | solution.py:15
  13.5 52.7 %collective-permute-start.3 = (bf16[192,2560]{1,0:T(8,128)(2,1)S(1)}, bf16[192,2560]{1,0:T(8,128)(2,1)}, u32[]{:S(2)}, u32[]{:S(2)}) collective-permute-start(bf16[192,2560]{1,0:T(8,128)(2,1)S(1)} %fusion.7), channel_id=1, source_target_pairs={{1,0},{2,1},{3,2},{4,3},{5,4},{6,5},{7,6},{8,7},{9,8},{10,9},{11,1... | collective-permute-start | bytes 2949128 | tf_op jit(solution)/shard_map/ppermute | solution.py:15
  15.4 84.4 %collective-permute-start = (bf16[192,2560]{1,0:T(8,128)(2,1)}, bf16[192,2560]{1,0:T(8,128)(2,1)}, u32[]{:S(2)}, u32[]{:S(2)}) collective-permute-start(bf16[192,2560]{1,0:T(8,128)(2,1)} %param.10), channel_id=1, source_target_pairs={{0,1},{1,2},{2,3},{3,4},{4,5},{5,6},{6,7},{7,8},{8,9},{9,10},{10,1... | collective-permute-start | bytes 2949128 | tf_op jit(solution)/shard_map/ppermute | solution.py:15
  19.1 82.4 %collective-permute-start.1 = (bf16[192,2560]{1,0:T(8,128)(2,1)}, bf16[192,2560]{1,0:T(8,128)(2,1)}, u32[]{:S(2)}, u32[]{:S(2)}) collective-permute-start(bf16[192,2560]{1,0:T(8,128)(2,1)} %param.10), channel_id=1, source_target_pairs={{1,0},{2,1},{3,2},{4,3},{5,4},{6,5},{7,6},{8,7},{9,8},{10,9},{11,1... | collective-permute-start | bytes 2949128 | tf_op jit(solution)/shard_map/ppermute | solution.py:15
  42.7 25.3 %copy-start.3 = (bf16[1,1,192,20,128]{4,2,1,3,0:T(8,128)(2,1)S(1)}, bf16[1,1,192,20,128]{4,2,1,3,0:T(8,128)(2,1)}, u32[]{:S(2)}) copy-start(bf16[1,1,192,20,128]{4,2,1,3,0:T(8,128)(2,1)} %copy.16) | copy-start | bytes 2949124
  68.0 1.7 copy-start.2
  68.1 1.7 copy-start.5
  103.2 4.5 %copy-start = (f32[20,192,3,192]{1,3,2,0:T(8,128)S(1)}, f32[20,192,3,192]{1,3,2,0:T(8,128)}, u32[]{:S(2)}) copy-start(f32[20,192,3,192]{1,3,2,0:T(8,128)} %get-tuple-element.6) | copy-start | bytes 26542084
  103.9 3.9 %copy-start.4 = (f32[20,192]{1,0:T(8,128)S(1)}, f32[20,192]{1,0:T(8,128)}, u32[]{:S(2)}) copy-start(f32[20,192]{1,0:T(8,128)} %get-tuple-element.5) | copy-start | bytes 46084
  109.5 73.6 %copy-start.7 = (f32[5120]{0:T(1024)S(1)}, f32[5120]{0:T(1024)}, u32[]{:S(2)}) copy-start(f32[5120]{0:T(1024)} %param.14) | copy-start | bytes 61444
Sparse Core Ops, SparseCore 0:
  8.9 174.0 all-gather.1
where the time goes:
time: 203 us
  waiting for transfers between devices  103 us (51%)
  local copies, waits for them, and re-layouts  28.4 us (14%)
  matrix products  24.2 us (12%)
  other arithmetic  20.4 us (10%)
  between operations  14.9 us (7%)
  starting transfers between devices  11.2 us (6%)
    all_gather x1, waiting for transfers between devices, local(): full_weight = lax.all_gather(out_weight, 'tm', axis=0, tiled=True)  67.5 us
    ppermute x4, waiting for transfers between devices, shifted(): return lax.ppermute(shard, axis, pairs)  35.3 us
    dot_general x1, matrix products, local(): jnp.dot(attended, full_weight, preferred_element_type=jnp.float32)  12.7 us
    reduce_max x1, other arithmetic, local(): top = jnp.max(logits, axis=-1, keepdims=True)  12.3 us
    reshape x1, local copies, waits for them, and re-layouts, local(): logits = logits.reshape(count, heads, tile, 3 * tile)  11.7 us
    ppermute x4, starting transfers between devices, shifted(): return lax.ppermute(shard, axis, pairs)  11.2 us
    another operation x6, local copies, waits for them, and re-layouts, local(): jnp.stack([key_buffer[offset:offset + count] for offset in range(3)], axi...  6.51 us
    unnamed x1, matrix products  6.05 us
  transfers between devices with their start and end apart: 5, of which 3 were waited for; matrix products, arithmetic and copies ran while one was open for 28% of the time, Pallas kernels for 0%

commit v1 on v0

--- a/solution.py
+++ b/solution.py
@@ -69,7 +69,9 @@
         preferred_element_type=jnp.float32,
     ).astype(jnp.bfloat16)
     attended = attended.reshape(rows, chans)
-    full_weight = lax.all_gather(out_weight, "tm", axis=0, tiled=True)
+    full_weight = jnp.concatenate(
+        lax.all_to_all(jnp.stack([out_weight] * lax.axis_size("tm")), "tm", 0, 0), axis=0
+    )
     projected = jnp.dot(attended, full_weight, preferred_element_type=jnp.float32)
     return (out_gate * projected).astype(jnp.bfloat16)
 

time: 203 us -> 661 us (3.26)
  the two profiles are of different devices: /device:TPU:27 before, /device:TPU:15 now
where the time goes in v1:
time: 661 us; the launch traced here: 660 us
  waiting for transfers between devices  558 us (84%)
  local copies, waits for them, and re-layouts  38.5 us (6%)
  matrix products  22.1 us (3%)
  other arithmetic  20.5 us (3%)
  starting transfers between devices  19.7 us (3%)
    ppermute x4, waiting for transfers between devices, shifted(): return lax.ppermute(shard, axis, pairs)  558 us
  transfers between devices with their start and end apart: 5, of which 2 were waited for; matrix products, arithmetic and copies ran while one was open for 9% of the time, Pallas kernels for 0%

profile of v1, /device:TPU:15, one launch (start us, length us, event | category | flops | bytes accessed | tf_op | source)
XLA Modules:
  0.0 660.0 jit_solution(12213975472313583493)
XLA Ops:
  0.0 9.7 %stack.67 = bf16[16,160,5120]{2,1,0:T(8,128)(2,1)} broadcast(bf16[160,5120]{1,0:T(8,128)(2,1)} %param.13), dimensions={1,2} | broadcast | bytes 27852800 | tf_op jit(solution)/shard_map/stack | solution.py:73
  9.7 6.7 %all-to-all-start = ((bf16[16,160,5120]{2,1,0:T(8,128)(2,1)}), bf16[16,160,5120]{2,1,0:T(8,128)(2,1)}, u32[]{:S(2)}, u32[]{:S(2)}) async-start(bf16[16,160,5120]{2,1,0:T(8,128)(2,1)} %stack.67), calls=%async_computation | async-start | bytes 52428800 | tf_op jit(solution)/shard_map/all_to_all | solution.py:73
  16.4 2.3 collective-permute-start.1
  18.7 4.2 collective-permute-start
  22.8 0.0 copy-done.1
  22.8 0.3 fusion.5
  23.1 0.0 copy-done.6
  23.1 1.2 fusion.7
  24.4 2.0 collective-permute-start.3
  26.4 4.5 collective-permute-start.2
  31.0 1.7 stack.27
  32.6 1.7 stack.64
  34.3 1.2 copy.16
  35.5 0.0 copy-done.8
  35.5 0.6 fusion.17
  37.3 0.1 add_bitcast_fusion
  37.4 0.0 copy-done.2
  37.4 0.3 fusion.2
  37.7 553.6 %collective-permute-done.1 = bf16[192,2560]{1,0:T(8,128)(2,1)} collective-permute-done((bf16[192,2560]{1,0:T(8,128)(2,1)}, bf16[192,2560]{1,0:T(8,128)(2,1)}, u32[]{:S(2)}, u32[]{:S(2)}) %collective-permute-start.1) | collective-permute-done | bytes 983072 | tf_op jit(solution)/shard_map/ppermute | solution.py:15
  591.2 1.7 stack.28
  592.9 0.0 collective-permute-done
  592.9 1.7 stack.26
  594.6 0.6 pad_maximum_fusion
  595.2 2.4 copy.14
  597.6 4.2 collective-permute-done.3
  601.8 1.7 stack.65
  603.4 0.0 copy-start.4
  603.5 0.2 copy.17
  603.7 0.0 collective-permute-done.2
  603.7 1.7 stack.63
  605.4 0.2 copy.15
  605.6 0.0 copy-done.4
  605.6 0.0 copy-start.3
  605.6 0.0 copy-start.7
  605.6 0.3 pad_maximum_fusion.1
  606.0 0.9 copy-done.3
  606.8 0.0 copy-done.7
  606.8 6.1 fusion.13
  612.9 11.4 %fusion.16 = (f32[20,192]{1,0:T(8,128)S(1)}, f32[20,192,3,192]{1,3,2,0:T(8,128)}) fusion(f32[20,192,3,192]{1,3,2,0:T(8,128)} %bitcast.38, pred[3]{0:T(512)(128)(4,1)S(1)} %add_bitcast_fusion), kind=kLoop, calls=%fused_computation.29 | loop fusion | flops 6631680 | bytes 17710084 | tf_op jit(solution)/shard_map/reduce_max | solution.py:62
  624.3 11.8 %copy.19 = f32[20,192,576]{2,1,0:T(8,128)} copy(f32[20,192,576]{1,2,0:T(8,128)} %bitcast.37) | data formatting | bytes 17694720 | tf_op jit(solution)/shard_map/reshape | solution.py:61
  636.1 6.3 exponential_reduce_fusion
  642.4 0.0 copy-done.5
  642.4 0.9 copy-done
  643.2 3.1 fusion.9
  646.3 0.7 copy.20
  647.0 0.0 all-to-all-done
  647.0 0.0 copy-done.9
  647.0 12.9 %fusion = bf16[192,5120]{1,0:T(8,128)(2,1)} fusion(bf16[2560,5120]{1,0:T(8,128)(2,1)} %bitcast.16, f32[5120]{0:T(1024)S(1)} %copy-done.9, bf16[24,8,20,128]{3,2,1,0:T(8,128)(2,1)S(1)} %bitcast.41), kind=kOutput, calls=%fused_computation.4 | convolution fusion | flops 5035130880 | bytes 29184000 | tf_op jit(solution)/shard_map/dot_general | solution.py:75
  (9 shorter events, 0.0 us)
Async XLA Ops:
  9.7 13.1 %copy-start.1 = (bf16[192,2560]{1,0:T(8,128)(2,1)S(1)}, bf16[192,2560]{1,0:T(8,128)(2,1)}, u32[]{:S(2)}) copy-start(bf16[192,2560]{1,0:T(8,128)(2,1)} %param.9) | copy-start | bytes 2949124
  9.7 13.4 %copy-start.6 = (f32[2560]{0:T(1024)S(1)}, f32[2560]{0:T(1024)}, u32[]{:S(2)}) copy-start(f32[2560]{0:T(1024)} %param.12) | copy-start | bytes 30724
  9.7 637.3 %all-to-all-start = ((bf16[16,160,5120]{2,1,0:T(8,128)(2,1)}), bf16[16,160,5120]{2,1,0:T(8,128)(2,1)}, u32[]{:S(2)}, u32[]{:S(2)}) async-start(bf16[16,160,5120]{2,1,0:T(8,128)(2,1)} %stack.67), calls=%async_computation | async-start | bytes 52428800 | tf_op jit(solution)/shard_map/all_to_all | solution.py:73
  16.4 574.9 %collective-permute-start.1 = (bf16[192,2560]{1,0:T(8,128)(2,1)}, bf16[192,2560]{1,0:T(8,128)(2,1)}, u32[]{:S(2)}, u32[]{:S(2)}) collective-permute-start(bf16[192,2560]{1,0:T(8,128)(2,1)} %param.10), channel_id=1, source_target_pairs={{1,0},{2,1},{3,2},{4,3},{5,4},{6,5},{7,6},{8,7},{9,8},{10,9},{11,1... | collective-permute-start | bytes 2949128 | tf_op jit(solution)/shard_map/ppermute | solution.py:15
  18.7 574.3 %collective-permute-start = (bf16[192,2560]{1,0:T(8,128)(2,1)}, bf16[192,2560]{1,0:T(8,128)(2,1)}, u32[]{:S(2)}, u32[]{:S(2)}) collective-permute-start(bf16[192,2560]{1,0:T(8,128)(2,1)} %param.10), channel_id=1, source_target_pairs={{0,1},{1,2},{2,3},{3,4},{4,5},{5,6},{6,7},{7,8},{8,9},{9,10},{10,1... | collective-permute-start | bytes 2949128 | tf_op jit(solution)/shard_map/ppermute | solution.py:15
  24.4 11.2 %copy-start.8 = (s32[1,2]{1,0:T(1,128)S(1)}, s32[1,2]{1,0:T(1,128)}, u32[]{:S(2)}) copy-start(s32[1,2]{1,0:T(1,128)} %param.15) | copy-start | bytes 28
  24.4 13.0 %copy-start.2 = (bf16[192,2560]{1,0:T(8,128)(2,1)S(1)}, bf16[192,2560]{1,0:T(8,128)(2,1)}, u32[]{:S(2)}) copy-start(bf16[192,2560]{1,0:T(8,128)(2,1)} %param.8) | copy-start | bytes 2949124
  24.4 577.4 %collective-permute-start.3 = (bf16[192,2560]{1,0:T(8,128)(2,1)}, bf16[192,2560]{1,0:T(8,128)(2,1)}, u32[]{:S(2)}, u32[]{:S(2)}) collective-permute-start(bf16[192,2560]{1,0:T(8,128)(2,1)} %fusion.7), channel_id=1, source_target_pairs={{1,0},{2,1},{3,2},{4,3},{5,4},{6,5},{7,6},{8,7},{9,8},{10,9},{11,1... | collective-permute-start | bytes 2949128 | tf_op jit(solution)/shard_map/ppermute | solution.py:15
  26.4 577.2 %collective-permute-start.2 = (bf16[192,2560]{1,0:T(8,128)(2,1)}, bf16[192,2560]{1,0:T(8,128)(2,1)}, u32[]{:S(2)}, u32[]{:S(2)}) collective-permute-start(bf16[192,2560]{1,0:T(8,128)(2,1)} %fusion.7), channel_id=1, source_target_pairs={{0,1},{1,2},{2,3},{3,4},{4,5},{5,6},{6,7},{7,8},{8,9},{9,10},{10,1... | collective-permute-start | bytes 2949128 | tf_op jit(solution)/shard_map/ppermute | solution.py:15
  603.4 2.2 copy-start.4
  605.6 1.2 copy-start.3
  605.6 1.2 copy-start.7
  624.3 18.1 %copy-start.5 = (bf16[1,3,192,20,128]{4,2,1,3,0:T(8,128)(2,1)S(1)}, bf16[1,3,192,20,128]{4,2,1,3,0:T(8,128)(2,1)}, u32[]{:S(2)}) copy-start(bf16[1,3,192,20,128]{4,2,1,3,0:T(8,128)(2,1)} %copy.14) | copy-start | bytes 8847364
  636.1 7.1 %copy-start = (f32[20,192,576]{2,1,0:T(8,128)S(1)}, f32[20,192,576]{2,1,0:T(8,128)}, u32[]{:S(2)}) copy-start(f32[20,192,576]{2,1,0:T(8,128)} %copy.19) | copy-start | bytes 26542084
  643.2 3.8 copy-start.9
